TPU v7x, 32 devices: a whole 2x2x4 slice. The times are simulated.
32 devices in a mesh: tm: 4 (over z), space: 8 (over y, x, core).
Axes of the slice: x: 2, y: 2, z: 4, core: 2. Of those that a mesh axis runs over, the one named last changes fastest.
Arguments:
- right_side: float32 [64, 2048, 128], P('space', 'tm'), may hold values from -3 to 3
- blocks: float32 [64, 7, 128, 128], P('space'), may hold values from -0.1875 to 0.1875
- neighbors: int32 [64, 7], P('space'), may hold values from 0 to 63, as said below
- shift_rates: float32 [4], replicated, may hold values from 5 to 8
Outputs:
- correction: float32 [64, 2048, 128], P('space', 'tm')
Inputs may be any that keep to these rules, and one draw needn't show every extreme that they name: The elements form planes of 8 consecutive elements. neighbors[e, 0] = e. With q the plane of e, column 1 names an element of plane q - 1 and column 2 one of plane q + 1, cyclically over the planes; within a plane, each of these two columns names every element of the neighbouring plane exactly once. Columns 3 to 6 name elements of plane q.
All inputs are finite; a program needn't handle non-finite values.
Results may differ from a plain program's by a relative error of at most 0.0003.
Values sent between devices are 32-bit elements; how exact they have to be, the bound alone decides.
A program may use at most 128 MiB of HBM per device.

v0:
```python
import functools
import math

import jax
import jax.numpy as jnp
from jax import lax
from jax.experimental import pallas as pl
from jax.experimental.pallas import tpu as pltpu
from jax.sharding import PartitionSpec as P

SWEEPS = 4
SLOTS = 7
PIECES = (4, 4, 4, 2, 1, 1)
CHUNKS = len(PIECES)
ROWS = 8
WRAP_WEIGHT = 0.01
DIAG_WEIGHT = 6.0
BLOCK_WEIGHT = 3.0
STEP_SCALE = 0.1
MESH = pl.DeviceIdType.MESH


def split(value):
    hi = value.astype(jnp.bfloat16)
    lo = (value - hi.astype(jnp.float32)).astype(jnp.bfloat16)
    return hi, lo


def windows(steps):
    unit = steps // sum(PIECES)
    return [(unit * sum(PIECES[:c]), unit * PIECES[c]) for c in range(CHUNKS)]


def kernel(
    tm_size, sp_size, x_ref, blocks_ref, near_ref, shift_ref,
    series_ref, table_ref, start_ref, *scratch
):
    plane, steps, nodes = x_ref.shape
    spans = windows(steps)
    moves = SWEEPS - 1
    zs = list(scratch[:SWEEPS])
    halos = scratch[SWEEPS : SWEEPS + 2 * moves * CHUNKS]
    (series, held, weights, table, gathered, own,
     send_sem, recv_sem, end_send, end_recv, load_sem, store_sem) = scratch[
        SWEEPS + 2 * moves * CHUNKS :
    ]
    tm = lax.axis_index("tm")
    sp = lax.axis_index("space")
    sides = (lax.rem(sp + 1, sp_size), lax.rem(sp + sp_size - 1, sp_size))
    peers = [lax.rem(tm + r, tm_size) for r in range(1, tm_size)]

    barrier = pltpu.get_barrier_semaphore()
    for side in sides:
        pl.semaphore_signal(barrier, inc=1, device_id={"space": side}, device_id_type=MESH)
    for peer in peers:
        pl.semaphore_signal(barrier, inc=1, device_id={"tm": peer}, device_id_type=MESH)
    load_blocks = pltpu.make_async_copy(blocks_ref, held, load_sem.at[0])
    load_x = pltpu.make_async_copy(x_ref, zs[0], load_sem.at[1])
    load_blocks.start()
    load_x.start()
    pl.semaphore_wait(barrier, 2 + len(peers))

    def near(e, s):
        return lax.rem(near_ref[e, s], plane)

    def halo(j, c, d):
        return halos[(j * CHUNKS + c) * 2 + d]

    def transfer(j, c, d):
        return pltpu.make_async_remote_copy(
            src_ref=(x_ref if j == 0 else zs[j]).at[:, pl.ds(*spans[c]), :],
            dst_ref=halo(j, c, d),
            send_sem=send_sem.at[j, c, d],
            recv_sem=recv_sem.at[j, c, d],
            device_id={"space": sides[d]},
            device_id_type=MESH,
        )

    for c in range(CHUNKS):
        for d in range(2):
            transfer(0, c, d).start()

    load_blocks.wait()

    def prepare(e, _):
        for s in range(SLOTS):
            hi, lo = split((-STEP_SCALE * BLOCK_WEIGHT) * held[e, s].T)
            weights[e, s * nodes : (s + 1) * nodes, :nodes] = hi
            weights[e, s * nodes : (s + 1) * nodes, nodes:] = lo
        return 0

    lax.fori_loop(0, plane, prepare, 0)

    sigmas = [STEP_SCALE * shift_ref[i] for i in range(SWEEPS)]
    rates = [1.0 / (1.0 + jnp.full((ROWS, nodes), sigma, jnp.float32)) for sigma in sigmas]

    def cascade(inputs, states):
        states = list(states)
        above = None
        for i in reversed(range(SWEEPS)):
            total = states[i] if inputs is None else inputs[i] + states[i]
            if above is not None:
                total = total + above
            states[i] = above = rates[i] * total
        return states

    row = lax.broadcasted_iota(jnp.int32, (ROWS, nodes), 0)
    unit = [(row == i).astype(jnp.float32) for i in range(SWEEPS)]

    def respond(g, states):
        kept = []
        for _ in range(ROWS):
            states = cascade(None, states)
            kept.append(states[0])
        flat = jnp.swapaxes(jnp.stack(kept), 0, 1)
        base = pl.multiple_of(g * ROWS, ROWS)
        for j in range(SWEEPS):
            table[j, pl.ds(base, ROWS), :] = flat[j]
        return tuple(states)

    over = lax.fori_loop(0, steps // ROWS, respond, tuple(unit))
    save_table = pltpu.make_async_copy(table, table_ref, store_sem.at[CHUNKS])
    save_table.start()
    carry_of = [[over[i][j : j + 1, :] for j in range(SWEEPS)] for i in range(SWEEPS)]

    def advance(vectors):
        result = []
        for i in range(SWEEPS):
            total = carry_of[i][i] * vectors[i]
            for j in range(i + 1, SWEEPS):
                total = total + carry_of[i][j] * vectors[j]
            result.append(total)
        return result

    around = list(over)
    for _ in range(tm_size - 1):
        around = advance(around)

    load_x.wait()
    def save(c):
        window = pl.ds(*spans[c])
        return pltpu.make_async_copy(
            series.at[:, window, :], series_ref.at[:, window, :], store_sem.at[c]
        )

    states = tuple(jnp.zeros((ROWS, nodes), jnp.float32) for _ in range(SWEEPS))
    for j in range(moves):
        diag = sigmas[j] - STEP_SCALE * DIAG_WEIGHT
        for c in range(CHUNKS):
            for d in range(2):
                transfer(j, c, d).wait_recv()
            first, width = spans[c]
            window = pl.ds(first, width)

            def apply(e, _):
                here = zs[j][e, window, :]
                parts = [
                    here,
                    halo(j, c, 0)[near(e, 1)],
                    halo(j, c, 1)[near(e, 2)],
                ] + [zs[j][near(e, s), window, :] for s in range(3, SLOTS)]
                pairs = [split(part) for part in parts]
                hi = jnp.concatenate([p[0] for p in pairs], axis=1)
                lo = jnp.concatenate([p[1] for p in pairs], axis=1)
                both = jnp.dot(hi, weights[e], preferred_element_type=jnp.float32)
                both = both + jnp.dot(lo, weights[e], preferred_element_type=jnp.float32)
                zs[j + 1][e, window, :] = diag * here + both[:, :nodes] + both[:, nodes:]
                return 0

            lax.fori_loop(0, plane, apply, 0)
            if j + 1 < moves:
                for d in range(2):
                    transfer(j + 1, c, d).start()
            else:

                def scan(g, states):
                    base = pl.multiple_of(first + g * ROWS, ROWS)
                    here = [jnp.swapaxes(z[:, pl.ds(base, ROWS), :], 0, 1) for z in zs]
                    kept = []
                    for t in range(ROWS):
                        states = cascade([h[t] for h in here], states)
                        kept.append(states[0])
                    series[:, pl.ds(base, ROWS), :] = jnp.swapaxes(jnp.stack(kept), 0, 1)
                    return tuple(states)

                states = lax.fori_loop(0, width // ROWS, scan, states)
                save(c).start()

    for i in range(SWEEPS):
        own[i] = states[i]
    ends = [
        pltpu.make_async_remote_copy(
            src_ref=own,
            dst_ref=gathered.at[r],
            send_sem=end_send.at[r],
            recv_sem=end_recv.at[r],
            device_id={"tm": peers[r]},
            device_id_type=MESH,
        )
        for r in range(tm_size - 1)
    ]
    for copy in ends:
        copy.start()
    for copy in ends:
        copy.wait()

    def enter(back):
        entered = lax.rem(tm - back + 1 + tm_size, tm_size)
        return jnp.where(entered == 0, jnp.float32(WRAP_WEIGHT), jnp.float32(1.0))

    total = [enter(tm_size) * own[i] for i in range(SWEEPS)]
    for back in range(tm_size - 1, 0, -1):
        moved = advance(total)
        total = [enter(back) * (gathered[back - 1, i] + moved[i]) for i in range(SWEEPS)]
    start = [None] * SWEEPS
    for i in reversed(range(SWEEPS)):
        value = total[i]
        for j in range(i + 1, SWEEPS):
            value = value + WRAP_WEIGHT * around[i][j : j + 1, :] * start[j]
        start[i] = value / (1.0 - WRAP_WEIGHT * around[i][i : i + 1, :])
    for e in range(plane):
        for i in range(SWEEPS):
            start_ref[e, i : i + 1, :] = start[i][e : e + 1, :]

    save_table.wait()
    for c in range(CHUNKS):
        save(c).wait()
    for j in range(moves):
        for c in range(CHUNKS):
            for d in range(2):
                transfer(j, c, d).wait_send()


def finish(series_ref, table_ref, start_ref, out_ref):
    steps = series_ref.shape[1]

    def some(g, _):
        rows = pl.ds(pl.multiple_of(g * 4 * ROWS, 4 * ROWS), 4 * ROWS)
        lines = [table_ref[i, rows, :] for i in range(SWEEPS)]
        for e in range(series_ref.shape[0]):
            value = series_ref[e, rows, :]
            for i in range(SWEEPS):
                value = value + lines[i] * start_ref[e, i : i + 1, :]
            out_ref[e, rows, :] = value
        return 0

    lax.fori_loop(0, steps // (4 * ROWS), some, 0)


def solution(mesh):
    tm_size, sp_size = mesh.shape["tm"], mesh.shape["space"]

    def per_device(right_side, blocks, neighbors, shift_rates):
        plane, steps, nodes = right_side.shape
        moves = SWEEPS - 1
        f32 = jnp.float32
        whole = pltpu.VMEM((plane, steps, nodes), f32)
        pieces = [pltpu.VMEM((plane, width, nodes), f32) for _, width in windows(steps)]
        dma = pltpu.SemaphoreType.DMA
        series, table, start = pl.pallas_call(
            functools.partial(kernel, tm_size, sp_size),
            out_shape=(
                jax.ShapeDtypeStruct(right_side.shape, f32),
                jax.ShapeDtypeStruct((SWEEPS, steps, nodes), f32),
                jax.ShapeDtypeStruct((plane, SWEEPS, nodes), f32),
            ),
            in_specs=[
                pl.BlockSpec(memory_space=pl.ANY),
                pl.BlockSpec(memory_space=pl.ANY),
                pl.BlockSpec(memory_space=pltpu.SMEM),
                pl.BlockSpec(memory_space=pltpu.SMEM),
            ],
            out_specs=(
                pl.BlockSpec(memory_space=pl.ANY),
                pl.BlockSpec(memory_space=pl.ANY),
                pl.BlockSpec(memory_space=pltpu.VMEM),
            ),
            scratch_shapes=[whole] * SWEEPS
            + [piece for _ in range(moves) for piece in pieces for _ in range(2)]
            + [
                whole,
                pltpu.VMEM(blocks.shape, f32),
                pltpu.VMEM((plane, SLOTS * nodes, 2 * nodes), jnp.bfloat16),
                pltpu.VMEM((SWEEPS, steps, nodes), f32),
                pltpu.VMEM((tm_size - 1, SWEEPS, plane, nodes), f32),
                pltpu.VMEM((SWEEPS, plane, nodes), f32),
                dma((moves, CHUNKS, 2)),
                dma((moves, CHUNKS, 2)),
                dma((tm_size - 1,)),
                dma((tm_size - 1,)),
                dma((2,)),
                dma((CHUNKS + 1,)),
            ],
            compiler_params=pltpu.CompilerParams(
                collective_id=0, has_side_effects=True, vmem_limit_bytes=60 * 2**20
            ),
        )(right_side, blocks, neighbors, shift_rates)
        block = pl.BlockSpec((2, steps, nodes), lambda e: (e, 0, 0))
        return pl.pallas_call(
            finish,
            grid=(plane // 2,),
            out_shape=jax.ShapeDtypeStruct(right_side.shape, f32),
            in_specs=[
                block,
                pl.BlockSpec((SWEEPS, steps, nodes), lambda e: (0, 0, 0)),
                pl.BlockSpec((2, SWEEPS, nodes), lambda e: (e, 0, 0)),
            ],
            out_specs=block,
        )(series, table, start)

    return jax.shard_map(
        per_device,
        mesh=mesh,
        in_specs=(P("space", "tm", None), P("space", None, None, None), P("space", None), P()),
        out_specs=P("space", "tm", None),
        check_vma=False,
    )
```

profile of v0, /device:TPU:9, one launch (start us, length us, event | category | flops | bytes accessed | tf_op | source)
XLA Modules:
  0.0 152.5 jit_solution(510404248844929884)
XLA Ops:
  0.0 147.8 %shard_map.46 = (f32[8,512,128]{2,1,0:T(8,128)}, f32[4,512,128]{2,1,0:T(8,128)}, f32[8,4,128]{2,1,0:T(4,128)}) custom-call(f32[8,512,128]{2,1,0:T(8,128)} %x_ref.1, f32[8,7,128,128]{3,2,1,0:T(8,128)} %blocks_ref.1, s32[8,7]{1,0:T(8,128)} %near_ref.1, f32[4]{0:T(128)} %shift_ref.1), custom_call_target="tpu_custom_call" | custom-call | tf_op jit(solution)/shard_map/pallas_call | solution.py:260
  147.8 4.7 %shard_map.47 = f32[8,512,128]{2,1,0:T(8,128)} custom-call(f32[8,512,128]{2,1,0:T(8,128)} %get-tuple-element.8.series_ref, f32[4,512,128]{2,1,0:T(8,128)} %get-tuple-element.9.table_ref, f32[8,4,128]{2,1,0:T(4,128)} %get-tuple-element.10.start_ref), custom_call_target="tpu_custom_call" | custom-call | tf_op jit(solution)/shard_map/pallas_call | solution.py:299
where the time goes:
time: 155 us; the launch traced here: 152 us
  Pallas kernels  152 us (98%)
    pallas_call x1, Pallas kernels, per_device(): pl.pallas_call(functools.partial(kernel, tm_size, sp_size), out_shape=(ja...  148 us
    pallas_call x1, Pallas kernels, per_device(): pl.pallas_call(finish, grid=(plane // 2,), out_shape=jax.ShapeDtypeStruct...  4.7 us

commit v1 on v0

v1 whole, which is shorter than its diff:
```python
import functools

import jax
import jax.numpy as jnp
from jax import lax
from jax.experimental import pallas as pl
from jax.experimental.pallas import tpu as pltpu
from jax.sharding import PartitionSpec as P

SWEEPS = 4
SLOTS = 7
PIECES = (2, 2, 2, 1, 1)
CHUNKS = len(PIECES)
ROWS = 8
WRAP_WEIGHT = 0.01
DIAG_WEIGHT = 6.0
BLOCK_WEIGHT = 3.0
STEP_SCALE = 0.1
MESH = pl.DeviceIdType.MESH


def split(value):
    hi = value.astype(jnp.bfloat16)
    lo = (value - hi.astype(jnp.float32)).astype(jnp.bfloat16)
    return hi, lo


def windows(half):
    unit = half // sum(PIECES)
    return [(unit * sum(PIECES[:c]), unit * PIECES[c]) for c in range(CHUNKS)]


def shares(tm_size, plane):
    counts = [plane // tm_size + (t < plane % tm_size) for t in range(tm_size)]
    for inner, outer in ((1, 0), (tm_size - 2, tm_size - 1)):
        if tm_size >= 4 and counts[inner] > 1:
            counts[inner] -= 1
            counts[outer] += 1
    owner = [t for t in range(tm_size) for _ in range(counts[t])]
    place = [sum(o == owner[e] for o in owner[:e]) for e in range(plane)]
    orders = [
        sorted(range(plane), key=lambda e: (place[e] + abs(owner[e] - t), abs(owner[e] - t)))
        for t in range(tm_size)
    ]
    return owner, orders


def kernel(
    tm_size, sp_size, x_ref, blocks_ref, near_ref, shift_ref,
    series_ref, table_ref, start_ref, *scratch
):
    plane, steps, nodes = x_ref.shape
    half = steps // 2
    spans = windows(half)
    moves = SWEEPS - 1
    groups = sp_size // 4
    segments = 2 * tm_size
    first_z = scratch[:CHUNKS]
    halos = scratch[CHUNKS : CHUNKS + 2 * moves * CHUNKS]
    (z1, z2, z3, series, held, weights, table, gathered, own, nearv, nears,
     w_recv, w_out, w_mate, w_fwd, d_recv, d_mate, d_out, n_recv, n_send, n_load,
     h_send, h_recv, r_send, r_recv, e_send, e_recv, t_store) = scratch[
        CHUNKS + 2 * moves * CHUNKS :
    ]
    zs = [None, z1, z2, z3]
    owner, orders = shares(tm_size, plane)
    tm = lax.axis_index("tm")
    sp = lax.axis_index("space")
    group = sp // 4
    chip = (sp // 2) % 2
    core = sp % 2
    far_side = (chip + core) % 2
    far = far_side == 1
    near = far_side == 0
    mate = group * 4 + chip * 2 + (1 - core)
    here_near = group * 4 + chip * 2 + chip
    there_far = group * 4 + (1 - chip) * 2 + chip
    across = ((group + groups + 2 * core - 1) % groups) * 4 + chip * 2 + (1 - core)

    def remote(src, dst, send, recv, **device):
        return pltpu.make_async_remote_copy(
            src_ref=src, dst_ref=dst, send_sem=send, recv_sem=recv,
            device_id=device, device_id_type=MESH,
        )

    def arrived(dst, recv):
        remote(dst, dst, n_send.at[0], recv, space=mate).wait_recv()

    barrier = pltpu.get_barrier_semaphore()
    greeted = 0
    for r in range(tm_size):
        for d in range(4):
            if r == 0 and d == 0:
                continue
            pl.semaphore_signal(
                barrier, inc=1, device_id_type=MESH,
                device_id={"tm": (tm + r) % tm_size, "space": group * 4 + (sp + d) % 4},
            )
            greeted += 1
    if groups > 1:
        pl.semaphore_signal(barrier, inc=1, device_id={"space": across}, device_id_type=MESH)
        greeted += 1

    def ranked(i):
        value = jnp.int32(orders[0][i])
        for t in range(1, tm_size):
            value = jnp.where(tm == t, jnp.int32(orders[t][i]), value)
        return value

    def owner_of(e):
        value = jnp.int32(owner[0])
        for k in range(1, plane):
            value = jnp.where(e == k, jnp.int32(owner[k]), value)
        return value

    def own_load(e):
        return pltpu.make_async_copy(blocks_ref.at[e], held.at[0, e], w_recv.at[0, e])

    def own_data(k):
        first, width = spans[k]
        return pltpu.make_async_copy(
            x_ref.at[:, pl.ds(chip * half + first, width), :], first_z[k].at[0], d_recv.at[k, 0]
        )

    def mate_data(k):
        first, width = spans[k]
        return remote(
            x_ref.at[:, pl.ds(chip * half + first, width), :], first_z[k].at[1],
            d_mate.at[k], d_recv.at[k, 1], space=mate,
        )

    def out_data(k):
        first, width = spans[k]
        return remote(
            x_ref.at[:, pl.ds((1 - chip) * half + first, width), :], first_z[k].at[far_side],
            d_out.at[k], d_recv.at[k, far_side], space=there_far,
        )

    def out_blocks(lp, e):
        return remote(
            blocks_ref.at[e] if lp == 0 else held.at[1, e], held.at[lp, e],
            w_out.at[lp, e], w_recv.at[lp, e], space=there_far,
        )

    def mate_blocks(e):
        return remote(
            blocks_ref.at[e], held.at[1, e], w_mate.at[e], w_recv.at[1, e], space=mate
        )

    def out_near():
        return remote(
            near_ref, nearv.at[far_side], n_send.at[0], n_recv.at[far_side], space=there_far
        )

    def mate_near():
        return remote(near_ref, nearv.at[1], n_send.at[1], n_recv.at[1], space=mate)

    def forward(lp, e, up):
        return remote(
            held.at[lp, e], held.at[lp, e], w_fwd.at[lp, e, up], w_recv.at[lp, e],
            tm=tm + 1 if up else tm - 1,
        )

    def forwards(lp, e, act):
        source = owner_of(e)

        @pl.when((tm <= source) & (tm > 0))
        def _():
            act(forward(lp, e, 0))

        @pl.when((tm >= source) & (tm < tm_size - 1))
        def _():
            act(forward(lp, e, 1))

    def halo(j, k, d):
        return halos[(j * CHUNKS + k) * 2 + d]

    def part(j, k, lp):
        if j == 0:
            return first_z[k].at[lp]
        return zs[j].at[lp, :, pl.ds(*spans[k]), :]

    def transfer(j, k, d):
        return remote(
            part(j, k, d), halo(j, k, d), h_send.at[j, k, d], h_recv.at[j, k, d],
            space=across if d == 0 else mate,
        )

    @pl.when(near)
    def _():
        for e in range(plane):
            own_load(e).start()
        for k in range(CHUNKS):
            own_data(k).start()
        pltpu.make_async_copy(near_ref, nearv.at[0], n_recv.at[0]).start()

    pl.semaphore_wait(barrier, greeted)

    @pl.when(near)
    def _():
        out_near().start()
        for e in range(plane):
            @pl.when(tm == owner[e])
            def _():
                out_blocks(0, e).start()

    @pl.when(far)
    def _():
        out_near().start()
        mate_near().start()
        for k in range(CHUNKS):
            mate_data(k).start()
        for i in range(plane):
            mate_blocks(ranked(i)).start()

    sigmas = [STEP_SCALE * shift_ref[i] for i in range(SWEEPS)]
    rates = [1.0 / (1.0 + jnp.full((ROWS, nodes), sigma, jnp.float32)) for sigma in sigmas]

    def cascade(inputs, states):
        states = list(states)
        above = None
        for i in reversed(range(SWEEPS)):
            total = states[i] if inputs is None else inputs[i] + states[i]
            if above is not None:
                total = total + above
            states[i] = above = rates[i] * total
        return states

    row = lax.broadcasted_iota(jnp.int32, (ROWS, nodes), 0)
    unit = [(row == i).astype(jnp.float32) for i in range(SWEEPS)]

    def respond(g, states):
        kept = []
        for _ in range(ROWS):
            states = cascade(None, states)
            kept.append(states[0])
        flat = jnp.swapaxes(jnp.stack(kept), 0, 1)
        base = pl.multiple_of(g * ROWS, ROWS)
        for j in range(SWEEPS):
            table[j, pl.ds(base, ROWS), :] = flat[j]
        return tuple(states)

    over = lax.fori_loop(0, half // ROWS, respond, tuple(unit))
    save_table = pltpu.make_async_copy(table, table_ref, t_store.at[0])
    save_table.start()
    carry_of = [[over[i][j : j + 1, :] for j in range(SWEEPS)] for i in range(SWEEPS)]

    def advance(vectors):
        result = []
        for i in range(SWEEPS):
            total = carry_of[i][i] * vectors[i]
            for j in range(i + 1, SWEEPS):
                total = total + carry_of[i][j] * vectors[j]
            result.append(total)
        return result

    around = list(over)
    for _ in range(segments - 1):
        around = advance(around)

    def prepare(lp, e):
        outer_slot = 1 + (core if lp == 0 else 1 - core)
        for b in range(SLOTS):
            s = outer_slot if b == 1 else 3 - outer_slot if b == 2 else b
            hi, lo = split((-STEP_SCALE * BLOCK_WEIGHT) * held[lp, e, s].T)
            weights[lp, e, b * nodes : (b + 1) * nodes, :nodes] = hi
            weights[lp, e, b * nodes : (b + 1) * nodes, nodes:] = lo

    def prepare_all(lp):
        def one(e, _):
            prepare(lp, e)
            return 0

        lax.fori_loop(0, plane, one, 0)

    @pl.when(near)
    def _():
        for i in range(plane):
            e = ranked(i)
            arrived(held.at[1, e], w_recv.at[1, e])

            @pl.when(tm == owner_of(e))
            def _():
                out_blocks(1, e).start()

        for k in range(CHUNKS):
            out_data(k).start()
        for k in range(CHUNKS):
            for lp in range(2):
                arrived(first_z[k].at[lp], d_recv.at[k, lp])
                transfer(0, k, lp).start()
        for e in range(plane):
            own_load(e).wait()
        prepare_all(0)
        prepare_all(1)

    def receive(lp, i):
        e = ranked(i)
        arrived(held.at[lp, e], w_recv.at[lp, e])
        forwards(lp, e, lambda copy: copy.start())
        return e

    @pl.when(far)
    def _():
        for i in range(plane):
            prepare(0, receive(0, i))

    for lp in range(2):
        arrived(nearv.at[lp], n_recv.at[lp])
    load_near = pltpu.make_async_copy(nearv, nears, n_load.at[0])
    load_near.start()
    load_near.wait()

    def apply(j, k, lp):
        first, width = spans[k]
        window = pl.ds(first, width)
        diag = sigmas[j] - STEP_SCALE * DIAG_WEIGHT
        outer_slot = 1 + (core if lp == 0 else 1 - core)

        def source(q, index):
            return first_z[k][q, index] if j == 0 else zs[j][q, index, window, :]

        def one(e, _):
            def near_of(s):
                return lax.rem(nears[lp, e, s], plane)

            here = source(lp, e)
            parts = [
                here,
                halo(j, k, lp)[near_of(outer_slot)],
                source(1 - lp, near_of(3 - outer_slot)),
            ] + [source(lp, near_of(s)) for s in range(3, SLOTS)]
            pairs = [split(p) for p in parts]
            hi = jnp.concatenate([p[0] for p in pairs], axis=1)
            lo = jnp.concatenate([p[1] for p in pairs], axis=1)
            both = jnp.dot(hi, weights[lp, e], preferred_element_type=jnp.float32)
            both = both + jnp.dot(lo, weights[lp, e], preferred_element_type=jnp.float32)
            zs[j + 1][lp, e, window, :] = diag * here + both[:, :nodes] + both[:, nodes:]
            return 0

        lax.fori_loop(0, plane, one, 0)

    due = [(plane * (k + 1)) // CHUNKS for k in range(CHUNKS)]
    shared = max(sum(o == t for o in owner) for t in range(tm_size))
    for k in range(CHUNKS):

        @pl.when(far)
        def _():
            for i in range(due[k - 1] if k else 0, due[k]):
                e = receive(1, i)
                if i == min(shared, due[0]) - 1:
                    for c in range(CHUNKS):
                        out_data(c).start()
                prepare(1, e)
            for lp in range(2):
                arrived(first_z[k].at[lp], d_recv.at[k, lp])
                transfer(0, k, lp).start()

        transfer(0, k, 0).wait_recv()
        apply(0, k, 0)
        transfer(1, k, 0).start()

    for k in range(CHUNKS):
        transfer(0, k, 1).wait_recv()
        apply(0, k, 1)
        transfer(1, k, 1).start()

    for k in range(CHUNKS):
        for lp in range(2):
            transfer(1, k, lp).wait_recv()
            apply(1, k, lp)
            transfer(2, k, lp).start()

    def back_target(lp):
        return group * 4 + 2 * core + (core + lp) % 2

    def give_back(k, lp):
        first, width = spans[k]
        return remote(
            series.at[lp, :, pl.ds(first, width), :],
            series_ref.at[:, pl.ds(chip * half + first, width), :],
            r_send.at[k, lp], r_recv.at[k, chip], space=back_target(lp),
        )

    def keep_back(k):
        first, width = spans[k]
        return pltpu.make_async_copy(
            series.at[0, :, pl.ds(first, width), :],
            series_ref.at[:, pl.ds(chip * half + first, width), :],
            r_recv.at[k, chip],
        )

    states = tuple(jnp.zeros((ROWS, nodes), jnp.float32) for _ in range(2 * SWEEPS))
    for k in range(CHUNKS):
        first, width = spans[k]
        for lp in range(2):
            transfer(2, k, lp).wait_recv()
            apply(2, k, lp)

        def scan(g, states):
            states = list(states)
            base = pl.multiple_of(first + g * ROWS, ROWS)
            inner = pl.multiple_of(g * ROWS, ROWS)
            for lp in range(2):
                mine = states[lp * SWEEPS : (lp + 1) * SWEEPS]
                here = [jnp.swapaxes(first_z[k][lp, :, pl.ds(inner, ROWS), :], 0, 1)] + [
                    jnp.swapaxes(z[lp, :, pl.ds(base, ROWS), :], 0, 1) for z in zs[1:]
                ]
                kept = []
                for t in range(ROWS):
                    mine = cascade([h[t] for h in here], mine)
                    kept.append(mine[0])
                series[lp, :, pl.ds(base, ROWS), :] = jnp.swapaxes(jnp.stack(kept), 0, 1)
                states[lp * SWEEPS : (lp + 1) * SWEEPS] = mine
            return tuple(states)

        states = lax.fori_loop(0, width // ROWS, scan, states)
        give_back(k, 1).start()

        @pl.when(far)
        def _():
            give_back(k, 0).start()

        @pl.when(near)
        def _():
            keep_back(k).start()

    for lp in range(2):
        for i in range(SWEEPS):
            own[lp, i] = states[lp * SWEEPS + i]
    segment = 2 * tm + chip

    def give_end(r, lp):
        return remote(
            own.at[lp], gathered.at[segment], e_send.at[r, lp], e_recv.at[segment],
            tm=(tm + r) % tm_size, space=back_target(lp),
        )

    for r in range(tm_size):
        for lp in range(2):
            if r == 0 and lp == 0:

                @pl.when(far)
                def _():
                    give_end(0, 0).start()

                @pl.when(near)
                def _():
                    pltpu.make_async_copy(
                        own.at[0], gathered.at[segment], e_recv.at[segment]
                    ).start()
            else:
                give_end(r, lp).start()
    for s in range(segments):
        arrived(gathered.at[s], e_recv.at[s])

    def ends(back):
        return [gathered[(2 * tm + segments - back) % segments, i] for i in range(SWEEPS)]

    def enter(back):
        entered = (2 * tm - back + 1 + segments) % segments
        return jnp.where(entered == 0, jnp.float32(WRAP_WEIGHT), jnp.float32(1.0))

    total = [enter(segments) * value for value in ends(segments)]
    for back in range(segments - 1, 0, -1):
        moved = advance(total)
        total = [enter(back) * (a + b) for a, b in zip(ends(back), moved)]
    start = [None] * SWEEPS
    for i in reversed(range(SWEEPS)):
        value = total[i]
        for j in range(i + 1, SWEEPS):
            value = value + WRAP_WEIGHT * around[i][j : j + 1, :] * start[j]
        start[i] = value / (1.0 - WRAP_WEIGHT * around[i][i : i + 1, :])
    later = [a + b for a, b in zip(ends(segments), advance(start))]
    for e in range(plane):
        for i in range(SWEEPS):
            start_ref[e, i : i + 1, :] = start[i][e : e + 1, :]
            start_ref[e, SWEEPS + i : SWEEPS + i + 1, :] = later[i][e : e + 1, :]

    save_table.wait()
    for k in range(CHUNKS):
        first, width = spans[k]
        for h in range(2):
            arrived(series_ref.at[:, pl.ds(h * half + first, width), :], r_recv.at[k, h])
    out_near().wait_send()
    for k in range(CHUNKS):
        out_data(k).wait_send()
        give_back(k, 1).wait_send()
        for j in range(moves):
            for d in range(2):
                transfer(j, k, d).wait_send()
    for r in range(tm_size):
        for lp in range(2):
            if r or lp:
                give_end(r, lp).wait_send()

    @pl.when(near)
    def _():
        for e in range(plane):
            @pl.when(tm == owner[e])
            def _():
                for lp in range(2):
                    out_blocks(lp, e).wait_send()

    @pl.when(far)
    def _():
        mate_near().wait_send()
        give_end(0, 0).wait_send()
        for k in range(CHUNKS):
            mate_data(k).wait_send()
            give_back(k, 0).wait_send()
        for e in range(plane):
            mate_blocks(e).wait_send()
            for lp in range(2):
                forwards(lp, e, lambda copy: copy.wait_send())


def finish(series_ref, table_ref, start_ref, out_ref):
    half = series_ref.shape[1] // 2

    def some(g, _):
        rows = pl.ds(pl.multiple_of(g * 4 * ROWS, 4 * ROWS), 4 * ROWS)
        lines = [table_ref[i, rows, :] for i in range(SWEEPS)]
        for h in range(2):
            place = pl.ds(pl.multiple_of(h * half + g * 4 * ROWS, 4 * ROWS), 4 * ROWS)
            for e in range(series_ref.shape[0]):
                value = series_ref[e, place, :]
                for i in range(SWEEPS):
                    row = h * SWEEPS + i
                    value = value + lines[i] * start_ref[e, row : row + 1, :]
                out_ref[e, place, :] = value
        return 0

    lax.fori_loop(0, half // (4 * ROWS), some, 0)


def solution(mesh):
    tm_size, sp_size = mesh.shape["tm"], mesh.shape["space"]

    def per_device(right_side, blocks, neighbors, shift_rates):
        plane, steps, nodes = right_side.shape
        half = steps // 2
        moves = SWEEPS - 1
        f32 = jnp.float32
        dma = pltpu.SemaphoreType.DMA
        whole = pltpu.VMEM((2, plane, half, nodes), f32)
        widths = [width for _, width in windows(half)]
        series, table, start = pl.pallas_call(
            functools.partial(kernel, tm_size, sp_size),
            out_shape=(
                jax.ShapeDtypeStruct(right_side.shape, f32),
                jax.ShapeDtypeStruct((SWEEPS, half, nodes), f32),
                jax.ShapeDtypeStruct((plane, 2 * SWEEPS, nodes), f32),
            ),
            in_specs=[
                pl.BlockSpec(memory_space=pl.ANY),
                pl.BlockSpec(memory_space=pl.ANY),
                pl.BlockSpec(memory_space=pl.ANY),
                pl.BlockSpec(memory_space=pltpu.SMEM),
            ],
            out_specs=(
                pl.BlockSpec(memory_space=pl.ANY),
                pl.BlockSpec(memory_space=pl.ANY),
                pl.BlockSpec(memory_space=pltpu.VMEM),
            ),
            scratch_shapes=[pltpu.VMEM((2, plane, width, nodes), f32) for width in widths]
            + [
                pltpu.VMEM((plane, width, nodes), f32)
                for _ in range(moves) for width in widths for _ in range(2)
            ]
            + [
                whole, whole, whole, whole,
                pltpu.VMEM((2,) + blocks.shape, f32),
                pltpu.VMEM((2, plane, SLOTS * nodes, 2 * nodes), jnp.bfloat16),
                pltpu.VMEM((SWEEPS, half, nodes), f32),
                pltpu.VMEM((2 * tm_size, SWEEPS, plane, nodes), f32),
                pltpu.VMEM((2, SWEEPS, plane, nodes), f32),
                pltpu.VMEM((2,) + neighbors.shape, jnp.int32),
                pltpu.SMEM((2,) + neighbors.shape, jnp.int32),
                dma((2, plane)),
                dma((2, plane)),
                dma((plane,)),
                dma((2, plane, 2)),
                dma((CHUNKS, 2)),
                dma((CHUNKS,)),
                dma((CHUNKS,)),
                dma((2,)),
                dma((2,)),
                dma((1,)),
                dma((moves, CHUNKS, 2)),
                dma((moves, CHUNKS, 2)),
                dma((CHUNKS, 2)),
                dma((CHUNKS, 2)),
                dma((tm_size, 2)),
                dma((2 * tm_size,)),
                dma((1,)),
            ],
            compiler_params=pltpu.CompilerParams(
                collective_id=0, has_side_effects=True, vmem_limit_bytes=60 * 2**20
            ),
        )(right_side, blocks, neighbors, shift_rates)
        block = pl.BlockSpec((2, steps, nodes), lambda e: (e, 0, 0))
        return pl.pallas_call(
            finish,
            grid=(plane // 2,),
            out_shape=jax.ShapeDtypeStruct(right_side.shape, f32),
            in_specs=[
                block,
                pl.BlockSpec((SWEEPS, half, nodes), lambda e: (0, 0, 0)),
                pl.BlockSpec((2, 2 * SWEEPS, nodes), lambda e: (e, 0, 0)),
            ],
            out_specs=block,
        )(series, table, start)

    return jax.shard_map(
        per_device,
        mesh=mesh,
        in_specs=(P("space", "tm", None), P("space", None, None, None), P("space", None), P()),
        out_specs=P("space", "tm", None),
        check_vma=False,
    )
```

time: 155 us -> 157 us (1.013)
  Pallas kernels: 152 us -> 155 us
    pallas_call x1, Pallas kernels: 148 us -> 151 us  [per_device(): pl.pallas_call(functools.partial(kernel, tm_size, sp_size), out_shape=(ja...]
where the time goes in v1:
time: 157 us; the launch traced here: 155 us
  Pallas kernels  155 us (99%)
    pallas_call x1, Pallas kernels, per_device(): pl.pallas_call(functools.partial(kernel, tm_size, sp_size), out_shape=(ja...  151 us
    pallas_call x1, Pallas kernels, per_device(): pl.pallas_call(finish, grid=(plane // 2,), out_shape=jax.ShapeDtypeStruct...  4.27 us

profile of v1, /device:TPU:9, one launch (start us, length us, event | category | flops | bytes accessed | tf_op | source)
XLA Modules:
  0.0 154.9 jit_solution(2784485261869133412)
XLA Ops:
  0.0 150.6 %shard_map.46 = (f32[8,512,128]{2,1,0:T(8,128)}, f32[4,256,128]{2,1,0:T(8,128)}, f32[8,8,128]{2,1,0:T(8,128)}) custom-call(f32[8,512,128]{2,1,0:T(8,128)} %x_ref.1, f32[8,7,128,128]{3,2,1,0:T(8,128)} %blocks_ref.1, s32[8,7]{1,0:T(8,128)} %near_ref.1, f32[4]{0:T(128)} %shift_ref.1), custom_call_target="tpu_custom_call" | custom-call | tf_op jit(solution)/shard_map/pallas_call | solution.py:548
  150.6 4.3 %shard_map.47 = f32[8,512,128]{2,1,0:T(8,128)} custom-call(f32[8,512,128]{2,1,0:T(8,128)} %get-tuple-element.8.series_ref, f32[4,256,128]{2,1,0:T(8,128)} %get-tuple-element.9.table_ref, f32[8,8,128]{2,1,0:T(8,128)} %get-tuple-element.10.start_ref), custom_call_target="tpu_custom_call" | custom-call | tf_op jit(solution)/shard_map/pallas_call | solution.py:603

commit v2 on v1

--- a/solution.py
+++ b/solution.py
@@ -9,7 +9,7 @@
 
 SWEEPS = 4
 SLOTS = 7
-PIECES = (2, 2, 2, 1, 1)
+PIECES = (2, 2, 2, 2)
 CHUNKS = len(PIECES)
 ROWS = 8
 WRAP_WEIGHT = 0.01
@@ -30,19 +30,31 @@
     return [(unit * sum(PIECES[:c]), unit * PIECES[c]) for c in range(CHUNKS)]
 
 
-def shares(tm_size, plane):
-    counts = [plane // tm_size + (t < plane % tm_size) for t in range(tm_size)]
-    for inner, outer in ((1, 0), (tm_size - 2, tm_size - 1)):
-        if tm_size >= 4 and counts[inner] > 1:
-            counts[inner] -= 1
-            counts[outer] += 1
-    owner = [t for t in range(tm_size) for _ in range(counts[t])]
-    place = [sum(o == owner[e] for o in owner[:e]) for e in range(plane)]
-    orders = [
-        sorted(range(plane), key=lambda e: (place[e] + abs(owner[e] - t), abs(owner[e] - t)))
-        for t in range(tm_size)
-    ]
-    return owner, orders
+def shares(plane):
+    ends = (3 * plane) // 8
+    rest = plane - ends
+    kinds = []
+    for lp in range(2):
+        low = (rest + 1 - lp) // 2
+        kinds.append([0] * ends + [1] * low + [2] * (rest - low))
+    return kinds
+
+
+def woven(kinds, lp):
+    ends = [(lp, e) for e in range(len(kinds)) if kinds[e] == 0]
+    low = [(lp, e) for e in range(len(kinds)) if kinds[e] == 1]
+    high = [(lp, e) for e in range(len(kinds)) if kinds[e] == 2]
+    middles = []
+    while low or high:
+        for side in (low, high) if lp == 0 else (high, low):
+            if side:
+                middles.append(side.pop(0))
+    order = list(middles[: 2 - lp])
+    for at, item in enumerate(ends):
+        order.append(item)
+        order += middles[2 - lp + at : 3 - lp + at]
+    order += middles[2 - lp + len(ends) :]
+    return middles, order
 
 
 def kernel(
@@ -63,7 +75,8 @@
         CHUNKS + 2 * moves * CHUNKS :
     ]
     zs = [None, z1, z2, z3]
-    owner, orders = shares(tm_size, plane)
+    kinds = shares(plane)
+    quad = tm_size % 4 == 0
     tm = lax.axis_index("tm")
     sp = lax.axis_index("space")
     group = sp // 4
@@ -72,6 +85,9 @@
     far_side = (chip + core) % 2
     far = far_side == 1
     near = far_side == 0
+    layer = tm % 4 if quad else tm * 0
+    middle = (layer == 1) | (layer == 2)
+    end = (layer == 0) | (layer == 3)
     mate = group * 4 + chip * 2 + (1 - core)
     here_near = group * 4 + chip * 2 + chip
     there_far = group * 4 + (1 - chip) * 2 + chip
@@ -101,17 +117,10 @@
         pl.semaphore_signal(barrier, inc=1, device_id={"space": across}, device_id_type=MESH)
         greeted += 1
 
-    def ranked(i):
-        value = jnp.int32(orders[0][i])
-        for t in range(1, tm_size):
-            value = jnp.where(tm == t, jnp.int32(orders[t][i]), value)
-        return value
-
-    def owner_of(e):
-        value = jnp.int32(owner[0])
-        for k in range(1, plane):
-            value = jnp.where(e == k, jnp.int32(owner[k]), value)
-        return value
+    def fetches(lp, e):
+        if not quad or kinds[lp][e] == 0:
+            return end
+        return layer == kinds[lp][e]
 
     def own_load(e):
         return pltpu.make_async_copy(blocks_ref.at[e], held.at[0, e], w_recv.at[0, e])
@@ -162,15 +171,15 @@
         )
 
     def forwards(lp, e, act):
-        source = owner_of(e)
-
-        @pl.when((tm <= source) & (tm > 0))
-        def _():
-            act(forward(lp, e, 0))
-
-        @pl.when((tm >= source) & (tm < tm_size - 1))
-        def _():
-            act(forward(lp, e, 1))
+        if not quad:
+            return
+        downs, ups = (((3,), (0,)), ((1,), (1, 2)), ((2, 1), (2,)))[kinds[lp][e]]
+        for way, layers in ((0, downs), (1, ups)):
+            for at in layers:
+
+                @pl.when(layer == at)
+                def _():
+                    act(forward(lp, e, way))
 
     def halo(j, k, d):
         return halos[(j * CHUNKS + k) * 2 + d]
@@ -196,22 +205,28 @@
 
     pl.semaphore_wait(barrier, greeted)
 
+    out_near().start()
+
+    @pl.when(end)
+    def _():
+        for k in range(CHUNKS):
+            out_data(k).start()
+
     @pl.when(near)
     def _():
-        out_near().start()
         for e in range(plane):
-            @pl.when(tm == owner[e])
+
+            @pl.when(fetches(0, e))
             def _():
                 out_blocks(0, e).start()
 
     @pl.when(far)
     def _():
-        out_near().start()
         mate_near().start()
         for k in range(CHUNKS):
             mate_data(k).start()
-        for i in range(plane):
-            mate_blocks(ranked(i)).start()
+        for e in range(plane):
+            mate_blocks(e).start()
 
     sigmas = [STEP_SCALE * shift_ref[i] for i in range(SWEEPS)]
     rates = [1.0 / (1.0 + jnp.full((ROWS, nodes), sigma, jnp.float32)) for sigma in sigmas]
@@ -275,16 +290,18 @@
 
     @pl.when(near)
     def _():
-        for i in range(plane):
-            e = ranked(i)
+        for e in range(plane):
             arrived(held.at[1, e], w_recv.at[1, e])
 
-            @pl.when(tm == owner_of(e))
+            @pl.when(fetches(1, e))
             def _():
                 out_blocks(1, e).start()
 
-        for k in range(CHUNKS):
-            out_data(k).start()
+        @pl.when(middle)
+        def _():
+            for k in range(CHUNKS):
+                out_data(k).start()
+
         for k in range(CHUNKS):
             for lp in range(2):
                 arrived(first_z[k].at[lp], d_recv.at[k, lp])
@@ -294,16 +311,37 @@
         prepare_all(0)
         prepare_all(1)
 
-    def receive(lp, i):
-        e = ranked(i)
+    def receive(lp, e):
         arrived(held.at[lp, e], w_recv.at[lp, e])
         forwards(lp, e, lambda copy: copy.start())
-        return e
+        prepare(lp, e)
+
+    between = [woven(kinds[lp], lp) for lp in range(2)]
+
+    @pl.when(far & middle)
+    def _():
+        ahead = between[0][0] + between[1][0]
+        for i, item in enumerate(ahead):
+            receive(*item)
+            if i == min(6, len(ahead) - 1):
+                for k in range(CHUNKS):
+                    out_data(k).start()
 
     @pl.when(far)
     def _():
-        for i in range(plane):
-            prepare(0, receive(0, i))
+        for k in range(CHUNKS):
+            for lp in range(2):
+                arrived(first_z[k].at[lp], d_recv.at[k, lp])
+                transfer(0, k, lp).start()
+
+    def receive_all(lp):
+        for _, e in between[lp][1]:
+
+            @pl.when(far & (end if kinds[lp][e] else layer >= 0))
+            def _():
+                receive(lp, e)
+
+    receive_all(0)
 
     for lp in range(2):
         arrived(nearv.at[lp], n_recv.at[lp])
@@ -333,40 +371,24 @@
             pairs = [split(p) for p in parts]
             hi = jnp.concatenate([p[0] for p in pairs], axis=1)
             lo = jnp.concatenate([p[1] for p in pairs], axis=1)
-            both = jnp.dot(hi, weights[lp, e], preferred_element_type=jnp.float32)
-            both = both + jnp.dot(lo, weights[lp, e], preferred_element_type=jnp.float32)
+            rows = jnp.concatenate([hi, lo], axis=0)
+            both = jnp.dot(rows, weights[lp, e], preferred_element_type=jnp.float32)
+            both = both[:width] + both[width:]
             zs[j + 1][lp, e, window, :] = diag * here + both[:, :nodes] + both[:, nodes:]
             return 0
 
-        lax.fori_loop(0, plane, one, 0)
-
-    due = [(plane * (k + 1)) // CHUNKS for k in range(CHUNKS)]
-    shared = max(sum(o == t for o in owner) for t in range(tm_size))
-    for k in range(CHUNKS):
-
-        @pl.when(far)
-        def _():
-            for i in range(due[k - 1] if k else 0, due[k]):
-                e = receive(1, i)
-                if i == min(shared, due[0]) - 1:
-                    for c in range(CHUNKS):
-                        out_data(c).start()
-                prepare(1, e)
-            for lp in range(2):
-                arrived(first_z[k].at[lp], d_recv.at[k, lp])
-                transfer(0, k, lp).start()
-
-        transfer(0, k, 0).wait_recv()
-        apply(0, k, 0)
-        transfer(1, k, 0).start()
-
-    for k in range(CHUNKS):
-        transfer(0, k, 1).wait_recv()
-        apply(0, k, 1)
-        transfer(1, k, 1).start()
-
-    for k in range(CHUNKS):
-        for lp in range(2):
+        lax.fori_loop(0, plane, one, 0, unroll=4)
+
+    for lp in range(2):
+        if lp == 1:
+            receive_all(1)
+        for k in range(CHUNKS):
+            transfer(0, k, lp).wait_recv()
+            apply(0, k, lp)
+            transfer(1, k, lp).start()
+
+    for lp in range(2):
+        for k in range(CHUNKS):
             transfer(1, k, lp).wait_recv()
             apply(1, k, lp)
             transfer(2, k, lp).start()
@@ -497,9 +519,10 @@
     @pl.when(near)
     def _():
         for e in range(plane):
-            @pl.when(tm == owner[e])
-            def _():
-                for lp in range(2):
+            for lp in range(2):
+
+                @pl.when(fetches(lp, e))
+                def _():
                     out_blocks(lp, e).wait_send()
 
     @pl.when(far)

time: 157 us -> 169 us (1.076); the launches traced: 155 us -> 169 us
  Pallas kernels: 155 us -> 169 us
    pallas_call x1, Pallas kernels: 151 us -> 165 us  [per_device(): pl.pallas_call(functools.partial(kernel, tm_size, sp_size), out_shape=(ja...]
where the time goes in v2:
time: 169 us
  Pallas kernels  169 us (100%)
    pallas_call x1, Pallas kernels, per_device(): pl.pallas_call(functools.partial(kernel, tm_size, sp_size), out_shape=(ja...  165 us
    pallas_call x1, Pallas kernels, per_device(): pl.pallas_call(finish, grid=(plane // 2,), out_shape=jax.ShapeDtypeStruct...  4.27 us

profile of v2, /device:TPU:9, one launch (start us, length us, event | category | flops | bytes accessed | tf_op | source)
XLA Modules:
  0.0 169.0 jit_solution(15712963669760093470)
XLA Ops:
  0.0 164.7 %shard_map.46 = (f32[8,512,128]{2,1,0:T(8,128)}, f32[4,256,128]{2,1,0:T(8,128)}, f32[8,8,128]{2,1,0:T(8,128)}) custom-call(f32[8,512,128]{2,1,0:T(8,128)} %x_ref.1, f32[8,7,128,128]{3,2,1,0:T(8,128)} %blocks_ref.1, s32[8,7]{1,0:T(8,128)} %near_ref.1, f32[4]{0:T(128)} %shift_ref.1), custom_call_target="tpu_custom_call" | custom-call | tf_op jit(solution)/shard_map/pallas_call | solution.py:571
  164.7 4.3 %shard_map.47 = f32[8,512,128]{2,1,0:T(8,128)} custom-call(f32[8,512,128]{2,1,0:T(8,128)} %get-tuple-element.8.series_ref, f32[4,256,128]{2,1,0:T(8,128)} %get-tuple-element.9.table_ref, f32[8,8,128]{2,1,0:T(8,128)} %get-tuple-element.10.start_ref), custom_call_target="tpu_custom_call" | custom-call | tf_op jit(solution)/shard_map/pallas_call | solution.py:626

commit v3 on v2

--- a/solution.py
+++ b/solution.py
@@ -311,21 +311,36 @@
         prepare_all(0)
         prepare_all(1)
 
-    def receive(lp, e):
+    def take(lp, e):
         arrived(held.at[lp, e], w_recv.at[lp, e])
         forwards(lp, e, lambda copy: copy.start())
-        prepare(lp, e)
 
     between = [woven(kinds[lp], lp) for lp in range(2)]
+    ends = sum(kind == 0 for kind in kinds[0])
+    for side in (1, 2):
+
+        @pl.when(far & (layer == side))
+        def _():
+            mine = [(lp, e) for lp in range(2) for e in range(plane) if kinds[lp][e] == side]
+            theirs = [(lp, e) for lp in range(2) for e in range(plane) if kinds[lp][e] == 3 - side]
+            for i in range(max(len(mine), len(theirs) + 2)):
+                if i < len(mine):
+                    take(*mine[i])
+                if i == len(mine) - 1:
+                    for k in range(CHUNKS):
+                        out_data(k).start()
+                if 0 <= i - 1 < len(theirs):
+                    take(*theirs[i - 1])
 
     @pl.when(far & middle)
     def _():
-        ahead = between[0][0] + between[1][0]
-        for i, item in enumerate(ahead):
-            receive(*item)
-            if i == min(6, len(ahead) - 1):
-                for k in range(CHUNKS):
-                    out_data(k).start()
+        for lp in range(2):
+
+            def one(e, _):
+                prepare(lp, e)
+                return 0
+
+            lax.fori_loop(ends, plane, one, 0)
 
     @pl.when(far)
     def _():
@@ -339,7 +354,8 @@
 
             @pl.when(far & (end if kinds[lp][e] else layer >= 0))
             def _():
-                receive(lp, e)
+                take(lp, e)
+                prepare(lp, e)
 
     receive_all(0)
 

time: 169 us -> 122 us (0.72)
  Pallas kernels: 169 us -> 121 us
    pallas_call x1, Pallas kernels: 165 us -> 117 us  [per_device(): pl.pallas_call(functools.partial(kernel, tm_size, sp_size), out_shape=(ja...]
where the time goes in v3:
time: 122 us; the launch traced here: 121 us
  Pallas kernels  121 us (99%)
    pallas_call x1, Pallas kernels, per_device(): pl.pallas_call(functools.partial(kernel, tm_size, sp_size), out_shape=(ja...  117 us
    pallas_call x1, Pallas kernels, per_device(): pl.pallas_call(finish, grid=(plane // 2,), out_shape=jax.ShapeDtypeStruct...  4.27 us

profile of v3, /device:TPU:9, one launch (start us, length us, event | category | flops | bytes accessed | tf_op | source)
XLA Modules:
  0.0 121.5 jit_solution(5966731531663564001)
XLA Ops:
  0.0 117.2 %shard_map.46 = (f32[8,512,128]{2,1,0:T(8,128)}, f32[4,256,128]{2,1,0:T(8,128)}, f32[8,8,128]{2,1,0:T(8,128)}) custom-call(f32[8,512,128]{2,1,0:T(8,128)} %x_ref.1, f32[8,7,128,128]{3,2,1,0:T(8,128)} %blocks_ref.1, s32[8,7]{1,0:T(8,128)} %near_ref.1, f32[4]{0:T(128)} %shift_ref.1), custom_call_target="tpu_custom_call" | custom-call | tf_op jit(solution)/shard_map/pallas_call | solution.py:587
  117.2 4.3 %shard_map.47 = f32[8,512,128]{2,1,0:T(8,128)} custom-call(f32[8,512,128]{2,1,0:T(8,128)} %get-tuple-element.8.series_ref, f32[4,256,128]{2,1,0:T(8,128)} %get-tuple-element.9.table_ref, f32[8,8,128]{2,1,0:T(8,128)} %get-tuple-element.10.start_ref), custom_call_target="tpu_custom_call" | custom-call | tf_op jit(solution)/shard_map/pallas_call | solution.py:642

commit v4 on v3

--- a/solution.py
+++ b/solution.py
@@ -9,7 +9,8 @@
 
 SWEEPS = 4
 SLOTS = 7
-PIECES = (2, 2, 2, 2)
+PIECES = (2, 2, 2, 1, 1)
+CUTS = ((0, 4), (4, 3))
 CHUNKS = len(PIECES)
 ROWS = 8
 WRAP_WEIGHT = 0.01
@@ -122,8 +123,13 @@
             return end
         return layer == kinds[lp][e]
 
-    def own_load(e):
-        return pltpu.make_async_copy(blocks_ref.at[e], held.at[0, e], w_recv.at[0, e])
+    def piece(ref, *place):
+        return ref.at[(*place[:-1], pl.ds(*CUTS[place[-1]]))]
+
+    def own_load(e, q):
+        return pltpu.make_async_copy(
+            piece(blocks_ref, e, q), piece(held, 0, e, q), w_recv.at[0, e, q]
+        )
 
     def own_data(k):
         first, width = spans[k]
@@ -145,15 +151,16 @@
             d_out.at[k], d_recv.at[k, far_side], space=there_far,
         )
 
-    def out_blocks(lp, e):
-        return remote(
-            blocks_ref.at[e] if lp == 0 else held.at[1, e], held.at[lp, e],
-            w_out.at[lp, e], w_recv.at[lp, e], space=there_far,
-        )
-
-    def mate_blocks(e):
-        return remote(
-            blocks_ref.at[e], held.at[1, e], w_mate.at[e], w_recv.at[1, e], space=mate
+    def out_blocks(lp, e, q):
+        return remote(
+            piece(blocks_ref, e, q) if lp == 0 else piece(held, 1, e, q), piece(held, lp, e, q),
+            w_out.at[lp, e, q], w_recv.at[lp, e, q], space=there_far,
+        )
+
+    def mate_blocks(e, q):
+        return remote(
+            piece(blocks_ref, e, q), piece(held, 1, e, q), w_mate.at[e, q], w_recv.at[1, e, q],
+            space=mate,
         )
 
     def out_near():
@@ -164,13 +171,13 @@
     def mate_near():
         return remote(near_ref, nearv.at[1], n_send.at[1], n_recv.at[1], space=mate)
 
-    def forward(lp, e, up):
-        return remote(
-            held.at[lp, e], held.at[lp, e], w_fwd.at[lp, e, up], w_recv.at[lp, e],
-            tm=tm + 1 if up else tm - 1,
-        )
-
-    def forwards(lp, e, act):
+    def forward(lp, e, q, up):
+        return remote(
+            piece(held, lp, e, q), piece(held, lp, e, q), w_fwd.at[lp, e, q, up],
+            w_recv.at[lp, e, q], tm=tm + 1 if up else tm - 1,
+        )
+
+    def forwards(lp, e, q, act):
         if not quad:
             return
         downs, ups = (((3,), (0,)), ((1,), (1, 2)), ((2, 1), (2,)))[kinds[lp][e]]
@@ -179,7 +186,7 @@
 
                 @pl.when(layer == at)
                 def _():
-                    act(forward(lp, e, way))
+                    act(forward(lp, e, q, way))
 
     def halo(j, k, d):
         return halos[(j * CHUNKS + k) * 2 + d]
@@ -198,7 +205,8 @@
     @pl.when(near)
     def _():
         for e in range(plane):
-            own_load(e).start()
+            for q in range(len(CUTS)):
+                own_load(e, q).start()
         for k in range(CHUNKS):
             own_data(k).start()
         pltpu.make_async_copy(near_ref, nearv.at[0], n_recv.at[0]).start()
@@ -218,7 +226,8 @@
 
             @pl.when(fetches(0, e))
             def _():
-                out_blocks(0, e).start()
+                for q in range(len(CUTS)):
+                    out_blocks(0, e, q).start()
 
     @pl.when(far)
     def _():
@@ -226,7 +235,8 @@
         for k in range(CHUNKS):
             mate_data(k).start()
         for e in range(plane):
-            mate_blocks(e).start()
+            for q in range(len(CUTS)):
+                mate_blocks(e, q).start()
 
     sigmas = [STEP_SCALE * shift_ref[i] for i in range(SWEEPS)]
     rates = [1.0 / (1.0 + jnp.full((ROWS, nodes), sigma, jnp.float32)) for sigma in sigmas]
@@ -291,11 +301,12 @@
     @pl.when(near)
     def _():
         for e in range(plane):
-            arrived(held.at[1, e], w_recv.at[1, e])
-
-            @pl.when(fetches(1, e))
-            def _():
-                out_blocks(1, e).start()
+            for q in range(len(CUTS)):
+                arrived(piece(held, 1, e, q), w_recv.at[1, e, q])
+
+                @pl.when(fetches(1, e))
+                def _():
+                    out_blocks(1, e, q).start()
 
         @pl.when(middle)
         def _():
@@ -307,13 +318,15 @@
                 arrived(first_z[k].at[lp], d_recv.at[k, lp])
                 transfer(0, k, lp).start()
         for e in range(plane):
-            own_load(e).wait()
+            for q in range(len(CUTS)):
+                own_load(e, q).wait()
         prepare_all(0)
         prepare_all(1)
 
     def take(lp, e):
-        arrived(held.at[lp, e], w_recv.at[lp, e])
-        forwards(lp, e, lambda copy: copy.start())
+        for q in range(len(CUTS)):
+            arrived(piece(held, lp, e, q), w_recv.at[lp, e, q])
+            forwards(lp, e, q, lambda copy: copy.start())
 
     between = [woven(kinds[lp], lp) for lp in range(2)]
     ends = sum(kind == 0 for kind in kinds[0])
@@ -395,19 +408,15 @@
 
         lax.fori_loop(0, plane, one, 0, unroll=4)
 
-    for lp in range(2):
-        if lp == 1:
-            receive_all(1)
-        for k in range(CHUNKS):
-            transfer(0, k, lp).wait_recv()
-            apply(0, k, lp)
-            transfer(1, k, lp).start()
-
-    for lp in range(2):
-        for k in range(CHUNKS):
-            transfer(1, k, lp).wait_recv()
-            apply(1, k, lp)
-            transfer(2, k, lp).start()
+    def move(j, k, lp):
+        transfer(j, k, lp).wait_recv()
+        apply(j, k, lp)
+        if j + 1 < moves:
+            transfer(j + 1, k, lp).start()
+
+    for k in range(CHUNKS):
+        move(0, k, 0)
+    receive_all(1)
 
     def back_target(lp):
         return group * 4 + 2 * core + (core + lp) % 2
@@ -429,11 +438,10 @@
         )
 
     states = tuple(jnp.zeros((ROWS, nodes), jnp.float32) for _ in range(2 * SWEEPS))
-    for k in range(CHUNKS):
+    def conclude(k, states):
         first, width = spans[k]
         for lp in range(2):
-            transfer(2, k, lp).wait_recv()
-            apply(2, k, lp)
+            move(2, k, lp)
 
         def scan(g, states):
             states = list(states)
@@ -463,6 +471,17 @@
         def _():
             keep_back(k).start()
 
+        return states
+
+    for k in range(CHUNKS + 2):
+        if k < CHUNKS:
+            move(0, k, 1)
+            move(1, k, 0)
+        if 0 <= k - 1 < CHUNKS:
+            move(1, k - 1, 1)
+        if k >= 2:
+            states = conclude(k - 2, states)
+
     for lp in range(2):
         for i in range(SWEEPS):
             own[lp, i] = states[lp * SWEEPS + i]
@@ -539,7 +558,8 @@
 
                 @pl.when(fetches(lp, e))
                 def _():
-                    out_blocks(lp, e).wait_send()
+                    for q in range(len(CUTS)):
+                        out_blocks(lp, e, q).wait_send()
 
     @pl.when(far)
     def _():
@@ -549,9 +569,10 @@
             mate_data(k).wait_send()
             give_back(k, 0).wait_send()
         for e in range(plane):
-            mate_blocks(e).wait_send()
-            for lp in range(2):
-                forwards(lp, e, lambda copy: copy.wait_send())
+            for q in range(len(CUTS)):
+                mate_blocks(e, q).wait_send()
+                for lp in range(2):
+                    forwards(lp, e, q, lambda copy: copy.wait_send())
 
 
 def finish(series_ref, table_ref, start_ref, out_ref):
@@ -616,10 +637,10 @@
                 pltpu.VMEM((2, SWEEPS, plane, nodes), f32),
                 pltpu.VMEM((2,) + neighbors.shape, jnp.int32),
                 pltpu.SMEM((2,) + neighbors.shape, jnp.int32),
-                dma((2, plane)),
-                dma((2, plane)),
-                dma((plane,)),
-                dma((2, plane, 2)),
+                dma((2, plane, len(CUTS))),
+                dma((2, plane, len(CUTS))),
+                dma((plane, len(CUTS))),
+                dma((2, plane, len(CUTS), 2)),
                 dma((CHUNKS, 2)),
                 dma((CHUNKS,)),
                 dma((CHUNKS,)),

time: 122 us -> 117 us (0.959)
  Pallas kernels: 121 us -> 117 us
    pallas_call x1, Pallas kernels: 117 us -> 113 us  [per_device(): pl.pallas_call(functools.partial(kernel, tm_size, sp_size), out_shape=(ja...]
where the time goes in v4:
time: 117 us
  Pallas kernels  117 us (100%)
    pallas_call x1, Pallas kernels, per_device(): pl.pallas_call(functools.partial(kernel, tm_size, sp_size), out_shape=(ja...  113 us
    pallas_call x1, Pallas kernels, per_device(): pl.pallas_call(finish, grid=(plane // 2,), out_shape=jax.ShapeDtypeStruct...  4.27 us

profile of v4, /device:TPU:9, one launch (start us, length us, event | category | flops | bytes accessed | tf_op | source)
XLA Modules:
  0.0 117.2 jit_solution(4312228307700161845)
XLA Ops:
  0.0 112.9 %shard_map.46 = (f32[8,512,128]{2,1,0:T(8,128)}, f32[4,256,128]{2,1,0:T(8,128)}, f32[8,8,128]{2,1,0:T(8,128)}) custom-call(f32[8,512,128]{2,1,0:T(8,128)} %x_ref.1, f32[8,7,128,128]{3,2,1,0:T(8,128)} %blocks_ref.1, s32[8,7]{1,0:T(8,128)} %near_ref.1, f32[4]{0:T(128)} %shift_ref.1), custom_call_target="tpu_custom_call" | custom-call | tf_op jit(solution)/shard_map/pallas_call | solution.py:608
  112.9 4.3 %shard_map.47 = f32[8,512,128]{2,1,0:T(8,128)} custom-call(f32[8,512,128]{2,1,0:T(8,128)} %get-tuple-element.8.series_ref, f32[4,256,128]{2,1,0:T(8,128)} %get-tuple-element.9.table_ref, f32[8,8,128]{2,1,0:T(8,128)} %get-tuple-element.10.start_ref), custom_call_target="tpu_custom_call" | custom-call | tf_op jit(solution)/shard_map/pallas_call | solution.py:663

commit v5 on v4

--- a/solution.py
+++ b/solution.py
@@ -32,10 +32,10 @@
 
 
 def shares(plane):
-    ends = (3 * plane) // 8
-    rest = plane - ends
     kinds = []
     for lp in range(2):
+        ends = (7 * plane + 8 * (1 - lp)) // 16
+        rest = plane - ends
         low = (rest + 1 - lp) // 2
         kinds.append([0] * ends + [1] * low + [2] * (rest - low))
     return kinds
@@ -329,7 +329,6 @@
             forwards(lp, e, q, lambda copy: copy.start())
 
     between = [woven(kinds[lp], lp) for lp in range(2)]
-    ends = sum(kind == 0 for kind in kinds[0])
     for side in (1, 2):
 
         @pl.when(far & (layer == side))
@@ -353,7 +352,7 @@
                 prepare(lp, e)
                 return 0
 
-            lax.fori_loop(ends, plane, one, 0)
+            lax.fori_loop(sum(kind == 0 for kind in kinds[lp]), plane, one, 0)
 
     @pl.when(far)
     def _():

time: 117 us -> 117 us (level)
  no operation moved by 1% of the time
where the time goes in v5:
time: 117 us; the launch traced here: 116 us
  Pallas kernels  116 us (99%)
    pallas_call x1, Pallas kernels, per_device(): pl.pallas_call(functools.partial(kernel, tm_size, sp_size), out_shape=(ja...  112 us
    pallas_call x1, Pallas kernels, per_device(): pl.pallas_call(finish, grid=(plane // 2,), out_shape=jax.ShapeDtypeStruct...  4.27 us

profile of v5, /device:TPU:9, one launch (start us, length us, event | category | flops | bytes accessed | tf_op | source)
XLA Modules:
  0.0 116.4 jit_solution(11862323148909999923)
XLA Ops:
  0.0 112.2 %shard_map.46 = (f32[8,512,128]{2,1,0:T(8,128)}, f32[4,256,128]{2,1,0:T(8,128)}, f32[8,8,128]{2,1,0:T(8,128)}) custom-call(f32[8,512,128]{2,1,0:T(8,128)} %x_ref.1, f32[8,7,128,128]{3,2,1,0:T(8,128)} %blocks_ref.1, s32[8,7]{1,0:T(8,128)} %near_ref.1, f32[4]{0:T(128)} %shift_ref.1), custom_call_target="tpu_custom_call" | custom-call | tf_op jit(solution)/shard_map/pallas_call | solution.py:607
  112.2 4.3 %shard_map.47 = f32[8,512,128]{2,1,0:T(8,128)} custom-call(f32[8,512,128]{2,1,0:T(8,128)} %get-tuple-element.8.series_ref, f32[4,256,128]{2,1,0:T(8,128)} %get-tuple-element.9.table_ref, f32[8,8,128]{2,1,0:T(8,128)} %get-tuple-element.10.start_ref), custom_call_target="tpu_custom_call" | custom-call | tf_op jit(solution)/shard_map/pallas_call | solution.py:662
